TPU v7x, 256 devices: a whole 4x4x8 slice. The times are simulated.
256 devices in a mesh: dp: 2 (over core), ctx: 16 (over z_hi, y), exp: 8 (over x, z_lo).
Axes of the slice: x: 4, y: 4, z: 8 (z_hi: 4, z_lo: 2; z = z_hi * 2 + z_lo), core: 2. Of those that a mesh axis runs over, the one named last changes fastest.
Arguments:
- tokens: bfloat16 [2, 2048, 2560], P('dp', 'ctx'), may hold values from -6 to 6
- queries: bfloat16 [2, 2048, 16, 576], P('dp', 'ctx', 'exp'), may hold values from -240 to 240
- kv_weight: bfloat16 [2560, 576], P('exp'), may hold values from -0.125 to 0.125
- kv_gain: bfloat16 [512], replicated, may hold values from 0.5 to 1.5
- uv_weight: bfloat16 [16, 512, 128], P('exp'), may hold values from -0.75 to 0.75
- out_weight: bfloat16 [2048, 2560], P('exp'), may hold values from -0.5 to 0.5
- post_gain: bfloat16 [2560], replicated, may hold values from 0.5 to 1.5
- router_weight: bfloat16 [2560, 32], replicated, may hold values from -0.125 to 0.125
- expert_ids: int32 [2, 2048, 6], P('dp', 'ctx'), may hold values from 0 to 31, all different within a row; in each aligned block of 128 rows (0 to 127, 128 to 255, ..., all dimensions but the last counted through in order) at most 32 rows name the same one
- doc_ids: int32 [2, 2048], P('dp', 'ctx'), may hold values from 0 to 3, never falling along the last dimension, each value on 1 to 1024 neighbouring positions
- gate_weight: bfloat16 [32, 2560, 1536], P('ctx', None, 'exp'), may hold values from -0.125 to 0.125
- up_weight: bfloat16 [32, 2560, 1536], P('ctx', None, 'exp'), may hold values from -0.125 to 0.125
- down_weight: bfloat16 [32, 1536, 2560], P('ctx', 'exp'), may hold values from -0.15625 to 0.15625
- cotangent: bfloat16 [2, 2048, 2560], P('dp', 'ctx'), may hold values from -6 to 6
Outputs:
- layer_out: bfloat16 [2, 2048, 2560], P('dp', 'ctx')
- router_grad: float32 [2560, 32], replicated
- gate_grad: bfloat16 [32, 2560, 1536], P('ctx', 'dp', 'exp')
- up_grad: bfloat16 [32, 2560, 1536], P('ctx', 'dp', 'exp')
- down_grad: bfloat16 [32, 1536, 2560], P('ctx', 'exp', 'dp')
Inputs may be any that keep to these rules, and one draw needn't show every extreme that they name: `expert_ids`: in each aligned block of 128 positions of a sequence no expert is named by more than 32 of the block's assignments; the experts of one token differ. `doc_ids`: document numbers never fall along a sequence; a document has at most 1024 positions.
All inputs are finite; a program needn't handle non-finite values.
Results may differ from a plain program's by a relative error of at most 0.023.
The roundings to bfloat16 on the way count: a program that leaves them out, or rounds other values in their place, can miss the bound.
Values may be sent and summed in bfloat16 or wider, within the bound.
No kernel may reach another device: no remote copies, remote signals or barrier semaphores. Data moves between devices by JAX's collectives and lax.ppermute only.
A program may use at most 128 MiB of HBM per device.

v0:
```python
import jax
import jax.numpy as jnp
from jax import lax
from jax.sharding import PartitionSpec as P

ROPE = 64
NOPE = 128
epsilon = 1e-06


def from_everyone(array, axis):
    count = lax.axis_size(axis)
    return lax.all_to_all(
        jnp.broadcast_to(array[None], (count, *array.shape)), axis, 0, 0, tiled=True
    )


def taken_together(array, axis):
    everything = from_everyone(array, axis)
    return jnp.sum(everything, axis=0)


def in_one_piece(arrays, axis, split_dim, concat_dim, along):
    both = jnp.concatenate(arrays, axis=along)
    result, at, gathered = (
        lax.all_to_all(both, axis, split_axis=split_dim, concat_axis=concat_dim, tiled=True),
        0,
        [],
    )
    for a in arrays:
        gathered.append(lax.slice_in_dim(result, at, at + a.shape[along], axis=along))
        at += a.shape[along]
    return tuple(gathered)


def rms_scale(values, gain):
    return values * lax.rsqrt(jnp.mean(values * values, axis=-1, keepdims=True) + epsilon) * gain


def rotate(rope_part, positions):
    half_width = rope_part.shape[-1] // 2
    frequency = jnp.power(
        10000.0, -2.0 * jnp.arange(half_width, dtype=jnp.float32) / rope_part.shape[-1]
    )
    angles = positions.astype(jnp.float32)[:, None] * frequency[None, :]
    cosine = jnp.cos(angles)
    sine_part = jnp.sin(angles)
    first_half = rope_part[:, :half_width]
    second = rope_part[:, half_width:]
    return jnp.concatenate(
        [first_half * cosine - second * sine_part, second * cosine + first_half * sine_part], axis=1
    )


def route_slots(outgoing):
    moved = lax.all_to_all(outgoing, ("dp", "ctx"), split_axis=0, concat_axis=0, tiled=True)
    return moved


def local(
    tokens,
    queries,
    kv_weight,
    kv_gain,
    uv_weight,
    out_weight,
    post_gain,
    router_weight,
    expert_ids,
    doc_ids,
    gate_weight,
    up_weight,
    down_weight,
    cotangent,
):
    local_rows = tokens[0]
    seq_rows = local_rows.shape[0]
    model_width = local_rows.shape[1]
    latent_width = kv_gain.shape[0]
    row_share = kv_weight.shape[0]
    columns = lax.dynamic_slice_in_dim(local_rows, lax.axis_index("exp") * row_share, row_share, 1)
    compressed = taken_together(
        jnp.dot(columns, kv_weight, preferred_element_type=jnp.float32), "exp"
    )
    positions = lax.axis_index("ctx") * seq_rows + jnp.arange(seq_rows, dtype=jnp.int32)
    latent = rms_scale(compressed[:, :latent_width], kv_gain.astype(jnp.float32)).astype(
        jnp.bfloat16
    )
    rope_key = rotate(compressed[:, latent_width:], positions).astype(jnp.bfloat16)
    key_rows = jnp.concatenate([latent, rope_key], axis=1)
    all_keys, all_docs = (
        lax.all_gather(key_rows, "ctx", axis=0, tiled=True),
        lax.all_gather(doc_ids[0], "ctx", axis=0, tiled=True),
    )
    key_positions = jnp.arange(all_keys.shape[0], dtype=jnp.int32)
    allowed = (key_positions[None, :] <= positions[:, None]) & (
        all_docs[None, :] == doc_ids[0][:, None]
    )
    allowed = allowed[:, None, :]
    score_scale = (NOPE + ROPE) ** (-0.5)
    scores = (
        jnp.einsum("qhd,kd->qhk", queries[0], all_keys, preferred_element_type=jnp.float32)
        * score_scale
    )
    score_peak = jnp.max(jnp.where(allowed, scores, -1e30), axis=-1, keepdims=True)
    weights = jnp.exp(jnp.where(allowed, scores - score_peak, -1e30))
    weight_total = jnp.sum(weights, axis=-1, keepdims=True)
    mixed_latent = (
        jnp.einsum(
            "qhk,kl->qhl",
            weights.astype(jnp.bfloat16),
            all_keys[:, :latent_width],
            preferred_element_type=jnp.float32,
        )
        / weight_total
    )
    mixed_latent = mixed_latent.astype(jnp.bfloat16)
    head_values = (
        jnp.einsum("qhl,hlv->qhv", mixed_latent, uv_weight, preferred_element_type=jnp.float32)
        .astype(jnp.bfloat16)
        .reshape(seq_rows, -1)
    )
    head_part = jnp.dot(head_values, out_weight, preferred_element_type=jnp.float32)
    attention = lax.psum(head_part, "exp")
    hidden = (local_rows.astype(jnp.float32) + attention).astype(jnp.bfloat16)
    normed = rms_scale(hidden.astype(jnp.float32), post_gain.astype(jnp.float32)).astype(
        jnp.bfloat16
    )
    logits = jnp.dot(normed, router_weight, preferred_element_type=jnp.float32)
    router_probs = jax.nn.softmax(logits, axis=-1)
    picked_ids = expert_ids[0]
    experts_all = router_weight.shape[1]
    top_count = picked_ids.shape[1]
    chosen = jnp.take_along_axis(router_probs, picked_ids, axis=1)
    chosen_sum = jnp.sum(chosen, axis=1, keepdims=True)
    route_w = chosen / chosen_sum
    route_wb = route_w.astype(jnp.bfloat16)
    ctx_count = lax.axis_size("ctx")
    held_experts = experts_all // ctx_count
    capacity = (4 * seq_rows * top_count + 3 * experts_all - 1) // (3 * experts_all)
    flat_ids = picked_ids.reshape(-1)
    onehot = (flat_ids[:, None] == jnp.arange(experts_all, dtype=jnp.int32)[None, :]).astype(
        jnp.int32
    )
    slot_rank = jnp.sum((jnp.cumsum(onehot, axis=0) - onehot) * onehot, axis=1).reshape(
        seq_rows, top_count
    )
    dp_count = lax.axis_size("dp")
    local_count = held_experts // dp_count
    first_local = lax.axis_index("dp") * local_count
    gate_local = lax.dynamic_slice_in_dim(gate_weight, first_local, local_count, 0)
    up_local = lax.dynamic_slice_in_dim(up_weight, first_local, local_count, 0)
    down_local = lax.dynamic_slice_in_dim(down_weight, first_local, local_count, 0)
    home_ctx = picked_ids // held_experts
    remainder = picked_ids % held_experts
    home_dp = remainder // local_count
    within = remainder % local_count
    slot_index = ((home_dp * ctx_count + home_ctx) * local_count + within) * capacity + slot_rank
    slot_hits = (
        slot_index[:, :, None] == jnp.arange(experts_all * capacity, dtype=jnp.int32)[None, None, :]
    )
    dispatch = jnp.any(slot_hits, axis=1).astype(jnp.bfloat16)
    combine = jnp.sum(
        jnp.where(slot_hits, route_wb[:, :, None], jnp.zeros((), jnp.bfloat16)), axis=1
    )
    outgoing = jnp.einsum("se,sd->ed", dispatch, normed, preferred_element_type=jnp.float32).astype(
        jnp.bfloat16
    )
    outgoing = outgoing.reshape(-1, local_count, capacity, model_width)
    arrived = route_slots(outgoing)
    gate_pre = jnp.einsum("sjcd,jdf->sjcf", arrived, gate_local, preferred_element_type=jnp.float32)
    up_pre = jnp.einsum("sjcd,jdf->sjcf", arrived, up_local, preferred_element_type=jnp.float32)
    activated = (jax.nn.silu(gate_pre) * up_pre).astype(jnp.bfloat16)
    expert_part = jnp.einsum(
        "sjcf,jfd->sjcd", activated, down_local, preferred_element_type=jnp.float32
    ).astype(jnp.bfloat16)
    returned = lax.all_to_all(expert_part, ("dp", "ctx"), split_axis=0, concat_axis=0, tiled=True)
    returned = returned.reshape(experts_all * capacity, model_width)
    moe_part = jnp.dot(combine, returned, preferred_element_type=jnp.float32)
    cot_rows = cotangent[0]
    cross_terms = jnp.einsum("sd,ed->se", cot_rows, returned, preferred_element_type=jnp.float32)
    dweight_part = jnp.take_along_axis(cross_terms, slot_index, axis=1)
    moe, dweight = lax.psum((moe_part, dweight_part), "exp")
    layer_out = (hidden.astype(jnp.float32) + moe).astype(jnp.bfloat16)
    mean_term = jnp.sum(dweight * route_w, axis=1, keepdims=True)
    dchosen = (dweight - mean_term) / chosen_sum
    id_hits = (
        picked_ids[:, :, None] == jnp.arange(experts_all, dtype=jnp.int32)[None, None, :]
    ).astype(jnp.float32)
    dprobs = jnp.sum(id_hits * dchosen[:, :, None], axis=1)
    dlogits = router_probs * (dprobs - jnp.sum(router_probs * dprobs, axis=1, keepdims=True))
    router_term = jnp.dot(normed.astype(jnp.float32).T, dlogits, precision=lax.Precision.HIGHEST)
    router_grad = lax.psum(router_term, ("dp", "ctx"))
    slot_cot = jnp.einsum(
        "se,sd->ed", combine, cot_rows, preferred_element_type=jnp.float32
    ).astype(jnp.bfloat16)
    slot_cot = slot_cot.reshape(-1, local_count, capacity, model_width)
    cot_arrived = route_slots(slot_cot)
    down_term = jnp.einsum(
        "sjcf,sjcd->jfd", activated, cot_arrived, preferred_element_type=jnp.float32
    )
    dact = jnp.einsum("sjcd,jfd->sjcf", cot_arrived, down_local, preferred_element_type=jnp.float32)
    sigmoid_gate = jax.nn.sigmoid(gate_pre)
    dgate = (dact * up_pre * sigmoid_gate * (1.0 + gate_pre * (1.0 - sigmoid_gate))).astype(
        jnp.bfloat16
    )
    dup = (dact * gate_pre * sigmoid_gate).astype(jnp.bfloat16)
    gate_term = jnp.einsum("sjcd,sjcf->jdf", arrived, dgate, preferred_element_type=jnp.float32)
    up_term = jnp.einsum("sjcd,sjcf->jdf", arrived, dup, preferred_element_type=jnp.float32)
    gate_out, up_out = in_one_piece(
        (gate_term.astype(jnp.bfloat16), up_term.astype(jnp.bfloat16)), "dp", 1, 0, 2
    )
    down_out = lax.all_to_all(
        down_term.astype(jnp.bfloat16), "dp", split_axis=2, concat_axis=0, tiled=True
    )
    return (layer_out[None], router_grad, gate_out, up_out, down_out)


def solution(mesh):
    placed = (
        P("dp", "ctx", None),
        P("dp", "ctx", "exp", None),
        P("exp", None),
        P(),
        P("exp", None, None),
        P("exp", None),
        P(),
        P(),
        P("dp", "ctx", None),
        P("dp", "ctx"),
        P("ctx", None, "exp"),
        P("ctx", None, "exp"),
        P("ctx", "exp", None),
        P("dp", "ctx", None),
    )
    return jax.shard_map(
        local,
        mesh=mesh,
        in_specs=placed,
        out_specs=(
            P("dp", "ctx", None),
            P(),
            P("ctx", "dp", "exp"),
            P("ctx", "dp", "exp"),
            P("ctx", "exp", "dp"),
        ),
        check_vma=False,
    )
```

profile of v0, /device:TPU:88, one launch (start us, length us, event | category | flops | bytes accessed | tf_op | source)
XLA Modules:
  0.0 998.6 jit_solution(10595866600486797685)
XLA Ops:
  10.4 5.8 all-to-all-start
  16.3 29.8 %all-to-all-done = f32[8,128,576]{1,2,0:T(8,128)} async-done(((f32[8,128,576]{1,2,0:T(8,128)}), f32[8,128,576]{1,2,0:T(8,128)}, u32[]{:S(2)}, u32[]{:S(2)}) %all-to-all-start) | async-done | bytes 2359328 | tf_op jit(solution)/shard_map/all_to_all | solution.py:13
  46.0 1.8 reduce_sum.102
  49.0 37.8 %all-gather = s32[1,2048]{1,0:T(1,128)S(1)} all-gather(s32[1,128]{1,0:T(1,128)S(1)} %copy-done.4), channel_id=2, replica_groups=mesh['dp'=2,'ctx'=16,'exp'=8] {'ctx'}, dimensions={1}, use_global_device_ids=true | all-gather | bytes 8704 | tf_op jit(solution)/shard_map/all_gather | solution.py:93
  87.1 26.5 %all-gather.3.cloned.1.call-done = bf16[2048,576]{0,1:T(8,128)(2,1)} async-done(((bf16[128,576]{0,1:T(8,128)(2,1)}), bf16[2048,576]{0,1:T(8,128)(2,1)}) %all-gather.3.cloned.1.call-update) | async-done | bytes 2359312 | tf_op jit(solution)/shard_map/all_gather | solution.py:92
  113.6 2.7 fusion.51
  116.3 1.9 fusion.156
  118.3 2.9 fusion.72
  123.1 1.7 reduce-window.6
  126.0 83.0 %all-reduce.4.cloned.1.call-done = f32[128,2560]{1,0:T(8,128)} async-done(((f32[128,2560]{1,0:T(8,128)}), f32[128,2560]{1,0:T(8,128)}) %all-reduce.4.cloned.1.call-update) | async-done | bytes 1310736 | tf_op jit(solution)/shard_map/psum | solution.py:124
  209.0 1.8 fusion.64
  210.8 3.9 convolution_convert_fusion.2
  214.7 8.9 all-to-all-start.1
  223.7 113.3 %all-to-all-done.1 = bf16[32,1,32,2560]{3,2,1,0:T(8,128)(2,1)} async-done(((bf16[32,1,32,2560]{3,2,1,0:T(8,128)(2,1)}), bf16[32,1,32,2560]{3,2,1,0:T(8,128)(2,1)}, u32[]{:S(2)}, u32[]{:S(2)}) %all-to-all-start.1) | async-done | bytes 5242912 | tf_op jit(solution)/shard_map/all_to_all | solution.py:56
  336.9 4.4 fusion.55
  341.4 5.4 multiply_convert_fusion.2
  347.6 3.8 fusion.13
  351.4 12.1 %all-to-all-start.2 = ((bf16[32,1,32,2560]{3,2,1,0:T(8,128)(2,1)}), bf16[32,1,32,2560]{3,2,1,0:T(8,128)(2,1)}, u32[]{:S(2)}, u32[]{:S(2)}) async-start(bf16[32,1,32,2560]{3,2,1,0:T(8,128)(2,1)} %fusion.13), calls=%async_computation.2 | async-start | bytes 10485760 | tf_op jit(solution)/shard_map/all_to_all | solution.py:177
  364.6 5.1 gather_fusion
  370.0 107.0 %all-to-all-done.2 = bf16[32,1,32,2560]{3,2,1,0:T(8,128)(2,1)} async-done(((bf16[32,1,32,2560]{3,2,1,0:T(8,128)(2,1)}), bf16[32,1,32,2560]{3,2,1,0:T(8,128)(2,1)}, u32[]{:S(2)}, u32[]{:S(2)}) %all-to-all-start.2) | async-done | bytes 5242912 | tf_op jit(solution)/shard_map/all_to_all | solution.py:177
  477.0 4.1 convolution_bitcast_fusion
  481.1 5.1 gather_fusion.1
  486.4 23.5 %psum.30 = f32[128,6]{0,1:T(8,128)S(1)} all-reduce(f32[128,6]{0,1:T(8,128)S(1)} %and_select_fusion), channel_id=1, replica_groups=mesh['dp'=2,'ctx'=16,'exp'=8] {'exp'}, use_global_device_ids=true, to_apply=%region_15.16 | all-reduce | flops 768 | bytes 6144 | tf_op jit(solution)/shard_map/psum | solution.py:183
  510.4 5.0 convolution_convert_fusion
  515.4 9.6 all-to-all-start.3
  525.0 4.4 fusion.159
  530.9 158.4 %all-reduce.6.cloned.1.call-done = f32[128,2560]{1,0:T(8,128)} async-done(((f32[128,2560]{1,0:T(8,128)}), f32[128,2560]{1,0:T(8,128)}) %all-reduce.6.cloned.1.call-update) | async-done | bytes 1310736 | tf_op jit(solution)/shard_map/psum | solution.py:183
  689.3 2.3 fusion.86
  691.6 4.1 fusion.61
  695.8 3.9 fusion.38
  699.6 3.8 fusion.35
  704.9 8.9 copy.117
  714.4 18.2 %reduce.3 = bf16[2560,384]{1,0:T(8,128)(2,1)} reduce(bf16[2560,1,384]{2,1,0:T(2,128)(2,1)} %bitcast.237, bf16[]{:T(256)} %broadcast.489), dimensions={1}, to_apply=%bitcast.212.reduce_sub_computation | reduce | bytes 3932162
  732.6 2.8 reshape.425
  735.3 8.4 all_to_all.50
  743.7 4.2 reshape.426
  748.0 2.5 copy.128
  750.5 4.7 fusion.32
  756.8 2.3 copy.120
  760.5 6.3 copy.118
  766.8 15.4 %reduce.4 = bf16[2560,192]{1,0:T(8,128)(2,1)S(1)} reduce(bf16[2560,1,192]{2,1,0:T(2,128)(2,1)} %bitcast.241, bf16[]{:T(256)} %broadcast.489), dimensions={1}, to_apply=%bitcast.214.reduce_sub_computation | reduce | bytes 1966082
  782.1 2.3 reshape.427
  784.5 5.6 all_to_all.51
  790.1 2.9 reshape.428
  793.0 5.1 copy.119
  799.3 2.2 copy.122
  801.5 188.8 %all-reduce.8.cloned.1.call-done = f32[2560,32]{0,1:T(8,128)} async-done(((f32[2560,32]{0,1:T(8,128)}), f32[2560,32]{0,1:T(8,128)}) %all-reduce.8.cloned.1.call-update) | async-done | bytes 327696 | tf_op jit(solution)/shard_map/psum | solution.py:193
  990.4 1.7 copy.146
  (88 shorter events, 17.9 us)
Async XLA Ops:
  7.2 340.4 %copy-start = (bf16[2,192,2560]{2,1,0:T(8,128)(2,1)S(1)}, bf16[2,192,2560]{2,1,0:T(8,128)(2,1)}, u32[]{:S(2)}) copy-start(bf16[2,192,2560]{2,1,0:T(8,128)(2,1)} %param.26) | copy-start | bytes 5898244
  10.4 5.9 copy-start.5
  10.4 35.7 %all-to-all-start = ((f32[8,128,576]{1,2,0:T(8,128)}), f32[8,128,576]{1,2,0:T(8,128)}, u32[]{:S(2)}, u32[]{:S(2)}) async-start(f32[8,128,576]{1,2,0:T(8,128)} %broadcast_in_dim.34), calls=%async_computation | async-start | bytes 4718592 | tf_op jit(solution)/shard_map/all_to_all | solution.py:13
  16.1 32.8 %copy-start.4 = (s32[1,128]{1,0:T(1,128)S(1)}, s32[1,128]{1,0:T(1,128)}, u32[]{:S(2)}) copy-start(s32[1,128]{1,0:T(1,128)} %param.23) | copy-start | bytes 1540
  16.2 97.5 %copy-start.7 = (bf16[1,128,2,576]{1,3,2,0:T(8,128)(2,1)S(1)}, bf16[1,128,2,576]{1,3,2,0:T(8,128)(2,1)}, u32[]{:S(2)}) copy-start(bf16[1,128,2,576]{1,3,2,0:T(8,128)(2,1)} %param.15) | copy-start | bytes 884740
  16.2 97.4 %all-gather.3.cloned.1.call-start = ((), (), s32[]{:S(2)}) async-start(), calls=%async_computation.6 | async-start | bytes 2506752 | tf_op jit(solution)/shard_map/all_gather | solution.py:92
  48.9 160.1 %all-reduce.4.cloned.1.call-start = ((), (), s32[]{:S(2)}) async-start(), calls=%async_computation.7 | async-start | bytes 2621440 | tf_op jit(solution)/shard_map/psum | solution.py:124
  118.3 2.9 copy-start.1
  121.2 1.5 copy-start.2
  121.2 4.3 copy-start.3
  214.7 122.2 %all-to-all-start.1 = ((bf16[32,1,32,2560]{3,2,1,0:T(8,128)(2,1)}), bf16[32,1,32,2560]{3,2,1,0:T(8,128)(2,1)}, u32[]{:S(2)}, u32[]{:S(2)}) async-start(bf16[32,1,32,2560]{3,2,1,0:T(8,128)(2,1)} %bitcast.235), calls=%async_computation.1 | async-start | bytes 10485760 | tf_op jit(solution)/shard_map/all_to_all | solution.py:56
  336.9 4.5 copy-start.6
  341.4 5.4 copy-start.9
  346.8 0.8 copy-start.12
  351.4 12.7 %copy-start.8 = (bf16[2560,32]{0,1:T(8,128)(2,1)S(1)}, bf16[2560,32]{0,1:T(8,128)(2,1)}, u32[]{:S(2)}) copy-start(bf16[2560,32]{0,1:T(8,128)(2,1)} %param.21) | copy-start | bytes 491524
  351.4 125.5 %all-to-all-start.2 = ((bf16[32,1,32,2560]{3,2,1,0:T(8,128)(2,1)}), bf16[32,1,32,2560]{3,2,1,0:T(8,128)(2,1)}, u32[]{:S(2)}, u32[]{:S(2)}) async-start(bf16[32,1,32,2560]{3,2,1,0:T(8,128)(2,1)} %fusion.13), calls=%async_computation.2 | async-start | bytes 10485760 | tf_op jit(solution)/shard_map/all_to_all | solution.py:177
  515.4 176.2 %all-to-all-start.3 = ((bf16[32,1,32,2560]{3,2,1,0:T(8,128)(2,1)}), bf16[32,1,32,2560]{3,2,1,0:T(8,128)(2,1)}, u32[]{:S(2)}, u32[]{:S(2)}) async-start(bf16[32,1,32,2560]{3,2,1,0:T(8,128)(2,1)} %bitcast.236), calls=%async_computation.3 | async-start | bytes 10485760 | tf_op jit(solution)/shard_map/all_to_all | solution.py:56
  525.0 164.4 %all-reduce.6.cloned.1.call-start = ((), (), s32[]{:S(2)}) async-start(), calls=%async_computation.8 | async-start | bytes 2621440 | tf_op jit(solution)/shard_map/psum | solution.py:183
  529.4 460.9 %all-reduce.8.cloned.1.call-start = ((), (), s32[]{:S(2)}) async-start(), calls=%async_computation.9 | async-start | bytes 655360 | tf_op jit(solution)/shard_map/psum | solution.py:193
  691.6 4.1 copy-start.10
  695.8 3.9 copy-start.11
  748.0 2.5 copy-start.13
Sparse Core Ops, SparseCore 0:
  49.1 64.4 all-gather.2
  122.8 86.1 all-reduce.3
  529.6 159.7 all-reduce.5
  692.4 297.9 all-reduce.7
where the time goes:
time: 1000 us; the launch traced here: 999 us
  waiting for transfers between devices  707 us (71%)
  blocking collectives  75.3 us (8%)
  local copies, waits for them, and re-layouts  60.3 us (6%)
  matrix products  58.1 us (6%)
  other arithmetic  47.3 us (5%)
  starting transfers between devices  36.6 us (4%)
  between operations  14.2 us (1%)
    psum x1, waiting for transfers between devices, local(): router_grad = lax.psum(router_term, ('dp', 'ctx'))  189 us
    psum x1, waiting for transfers between devices, local(): moe, dweight = lax.psum((moe_part, dweight_part), 'exp')  158 us
    all_to_all x2, waiting for transfers between devices, route_slots(): lax.all_to_all(outgoing, ('dp', 'ctx'), split_axis=0, concat_axis=0, tile...  113 us
    all_to_all x1, waiting for transfers between devices, local(): lax.all_to_all(expert_part, ('dp', 'ctx'), split_axis=0, concat_axis=0, t...  107 us
    psum x1, waiting for transfers between devices, local(): attention = lax.psum(head_part, 'exp')  83 us
    all_gather x1, blocking collectives, local(): lax.all_gather(doc_ids[0], 'ctx', axis=0, tiled=True)  37.8 us
    unnamed x2, other arithmetic  33.5 us
    all_to_all x1, waiting for transfers between devices, from_everyone(): lax.all_to_all(jnp.broadcast_to(array[None], (count, *array.shape)), axis...  29.8 us
  transfers between devices with their start and end apart: 8, of which 7 were waited for; matrix products, arithmetic and copies ran while one was open for 11% of the time, Pallas kernels for 0%

commit v1 on v0

--- a/solution.py
+++ b/solution.py
@@ -1,11 +1,20 @@
+import functools
 import jax
 import jax.numpy as jnp
 from jax import lax
 from jax.sharding import PartitionSpec as P
+from jax.lax import psum
 
 ROPE = 64
 NOPE = 128
 epsilon = 1e-06
+
+
+def _link_columns(mine, axis_name, along_axis):
+    return psum(psum(mine, axis_name=axis_name), axis_name=along_axis)
+
+
+track_units = functools.partial(_link_columns, axis_name="ctx", along_axis="dp")
 
 
 def from_everyone(array, axis):
@@ -190,7 +199,7 @@
     dprobs = jnp.sum(id_hits * dchosen[:, :, None], axis=1)
     dlogits = router_probs * (dprobs - jnp.sum(router_probs * dprobs, axis=1, keepdims=True))
     router_term = jnp.dot(normed.astype(jnp.float32).T, dlogits, precision=lax.Precision.HIGHEST)
-    router_grad = lax.psum(router_term, ("dp", "ctx"))
+    router_grad = track_units(router_term)
     slot_cot = jnp.einsum(
         "se,sd->ed", combine, cot_rows, preferred_element_type=jnp.float32
     ).astype(jnp.bfloat16)

time: 1000 us -> 947 us (0.947)
  waiting for transfers between devices: 707 us -> 651 us
    psum x1, waiting for transfers between devices: 158 us -> 89 us  [local(): moe, dweight = lax.psum((moe_part, dweight_part), 'exp')]
    psum x1 -> x2, waiting for transfers between devices: 189 us -> 203 us  [_link_columns(): return psum(psum(mine, axis_name=axis_name), axis_name=along_axis)]
  transfers between devices with their start and end apart: 8 -> 9, of which waited for: 7 -> 7; matrix products, arithmetic and copies ran while one was open for 11% -> 12% of each run, Pallas kernels for 0% -> 0%
where the time goes in v1:
time: 947 us; the launch traced here: 943 us
  waiting for transfers between devices  651 us (69%)
  blocking collectives  75.3 us (8%)
  local copies, waits for them, and re-layouts  60.3 us (6%)
  matrix products  58 us (6%)
  other arithmetic  47.4 us (5%)
  starting transfers between devices  36.6 us (4%)
  between operations  14.3 us (2%)
    psum x2, waiting for transfers between devices, _link_columns(): return psum(psum(mine, axis_name=axis_name), axis_name=along_axis)  203 us
    all_to_all x2, waiting for transfers between devices, route_slots(): lax.all_to_all(outgoing, ('dp', 'ctx'), split_axis=0, concat_axis=0, tile...  113 us
    all_to_all x1, waiting for transfers between devices, local(): lax.all_to_all(expert_part, ('dp', 'ctx'), split_axis=0, concat_axis=0, t...  107 us
    psum x1, waiting for transfers between devices, local(): moe, dweight = lax.psum((moe_part, dweight_part), 'exp')  89 us
    psum x1, waiting for transfers between devices, local(): attention = lax.psum(head_part, 'exp')  83 us
    all_gather x1, blocking collectives, local(): lax.all_gather(doc_ids[0], 'ctx', axis=0, tiled=True)  37.8 us
    unnamed x2, other arithmetic  33.6 us
    all_to_all x1, waiting for transfers between devices, from_everyone(): lax.all_to_all(jnp.broadcast_to(array[None], (count, *array.shape)), axis...  29.8 us
  transfers between devices with their start and end apart: 9, of which 7 were waited for; matrix products, arithmetic and copies ran while one was open for 12% of the time, Pallas kernels for 0%

profile of v1, /device:TPU:88, one launch (start us, length us, event | category | flops | bytes accessed | tf_op | source)
XLA Modules:
  0.0 942.9 jit_solution(2001715051286146553)
XLA Ops:
  10.4 5.8 all-to-all-start
  16.3 29.8 %all-to-all-done = f32[8,128,576]{1,2,0:T(8,128)} async-done(((f32[8,128,576]{1,2,0:T(8,128)}), f32[8,128,576]{1,2,0:T(8,128)}, u32[]{:S(2)}, u32[]{:S(2)}) %all-to-all-start) | async-done | bytes 2359328 | tf_op jit(solution)/shard_map/all_to_all | solution.py:22
  46.0 1.8 reduce_sum.102
  49.0 37.8 %all-gather = s32[1,2048]{1,0:T(1,128)S(1)} all-gather(s32[1,128]{1,0:T(1,128)S(1)} %copy-done.4), channel_id=2, replica_groups=mesh['dp'=2,'ctx'=16,'exp'=8] {'ctx'}, dimensions={1}, use_global_device_ids=true | all-gather | bytes 8704 | tf_op jit(solution)/shard_map/all_gather | solution.py:102
  87.1 26.5 %all-gather.3.cloned.1.call-done = bf16[2048,576]{0,1:T(8,128)(2,1)} async-done(((bf16[128,576]{0,1:T(8,128)(2,1)}), bf16[2048,576]{0,1:T(8,128)(2,1)}) %all-gather.3.cloned.1.call-update) | async-done | bytes 2359312 | tf_op jit(solution)/shard_map/all_gather | solution.py:101
  113.6 2.7 fusion.51
  116.3 1.9 fusion.156
  118.3 2.9 fusion.72
  123.1 1.7 reduce-window.6
  126.0 83.0 %all-reduce.5.cloned.1.call-done = f32[128,2560]{1,0:T(8,128)} async-done(((f32[128,2560]{1,0:T(8,128)}), f32[128,2560]{1,0:T(8,128)}) %all-reduce.5.cloned.1.call-update) | async-done | bytes 1310736 | tf_op jit(solution)/shard_map/psum | solution.py:133
  209.0 1.8 fusion.64
  210.8 3.9 convolution_convert_fusion.2
  214.7 8.9 all-to-all-start.1
  223.7 113.3 %all-to-all-done.1 = bf16[32,1,32,2560]{3,2,1,0:T(8,128)(2,1)} async-done(((bf16[32,1,32,2560]{3,2,1,0:T(8,128)(2,1)}), bf16[32,1,32,2560]{3,2,1,0:T(8,128)(2,1)}, u32[]{:S(2)}, u32[]{:S(2)}) %all-to-all-start.1) | async-done | bytes 5242912 | tf_op jit(solution)/shard_map/all_to_all | solution.py:65
  336.9 4.4 fusion.55
  341.4 5.4 multiply_convert_fusion.2
  347.6 3.8 fusion.13
  351.4 12.1 %all-to-all-start.2 = ((bf16[32,1,32,2560]{3,2,1,0:T(8,128)(2,1)}), bf16[32,1,32,2560]{3,2,1,0:T(8,128)(2,1)}, u32[]{:S(2)}, u32[]{:S(2)}) async-start(bf16[32,1,32,2560]{3,2,1,0:T(8,128)(2,1)} %fusion.13), calls=%async_computation.2 | async-start | bytes 10485760 | tf_op jit(solution)/shard_map/all_to_all | solution.py:186
  364.6 5.1 gather_fusion
  370.0 107.0 %all-to-all-done.2 = bf16[32,1,32,2560]{3,2,1,0:T(8,128)(2,1)} async-done(((bf16[32,1,32,2560]{3,2,1,0:T(8,128)(2,1)}), bf16[32,1,32,2560]{3,2,1,0:T(8,128)(2,1)}, u32[]{:S(2)}, u32[]{:S(2)}) %all-to-all-start.2) | async-done | bytes 5242912 | tf_op jit(solution)/shard_map/all_to_all | solution.py:186
  477.0 4.1 convolution_bitcast_fusion
  481.1 5.1 gather_fusion.1
  486.4 23.5 %psum.37 = f32[128,6]{0,1:T(8,128)S(1)} all-reduce(f32[128,6]{0,1:T(8,128)S(1)} %and_select_fusion), channel_id=1, replica_groups=mesh['dp'=2,'ctx'=16,'exp'=8] {'exp'}, use_global_device_ids=true, to_apply=%region_15.16 | all-reduce | flops 768 | bytes 6144 | tf_op jit(solution)/shard_map/psum | solution.py:192
  510.4 5.0 convolution_convert_fusion
  515.4 9.6 %all-to-all-start.3 = ((bf16[32,1,32,2560]{3,2,1,0:T(8,128)(2,1)}), bf16[32,1,32,2560]{3,2,1,0:T(8,128)(2,1)}, u32[]{:S(2)}, u32[]{:S(2)}) async-start(bf16[32,1,32,2560]{3,2,1,0:T(8,128)(2,1)} %bitcast.236), calls=%async_computation.3 | async-start | bytes 10485760 | tf_op jit(solution)/shard_map/all_to_all | solution.py:65
  526.4 4.4 fusion.159
  530.9 202.5 %all-reduce.9.cloned.1.call-done = f32[2560,32]{0,1:T(8,128)} async-done(((f32[2560,32]{0,1:T(8,128)}), f32[2560,32]{0,1:T(8,128)}) %all-reduce.9.cloned.1.call-update) | async-done | bytes 327696 | tf_op jit(solution)/shard_map/psum | solution.py:14
  733.5 89.0 %all-reduce.7.cloned.1.call-done = f32[128,2560]{1,0:T(8,128)} async-done(((f32[128,2560]{1,0:T(8,128)}), f32[128,2560]{1,0:T(8,128)}) %all-reduce.7.cloned.1.call-update) | async-done | bytes 1310736 | tf_op jit(solution)/shard_map/psum | solution.py:192
  822.5 2.3 fusion.86
  824.8 4.1 fusion.61
  828.9 3.9 fusion.38
  832.8 3.8 fusion.35
  838.0 8.9 copy.117
  847.5 18.2 %reduce.3 = bf16[2560,384]{1,0:T(8,128)(2,1)} reduce(bf16[2560,1,384]{2,1,0:T(2,128)(2,1)} %bitcast.237, bf16[]{:T(256)} %broadcast.489), dimensions={1}, to_apply=%bitcast.212.reduce_sub_computation | reduce | bytes 3932162
  865.7 2.8 reshape.425
  868.5 8.4 all_to_all.50
  876.9 4.2 reshape.426
  881.1 2.5 copy.128
  883.6 4.6 fusion.32
  889.9 2.3 copy.120
  893.5 6.3 copy.118
  899.9 15.4 %reduce.4 = bf16[2560,192]{1,0:T(8,128)(2,1)S(1)} reduce(bf16[2560,1,192]{2,1,0:T(2,128)(2,1)} %bitcast.241, bf16[]{:T(256)} %broadcast.489), dimensions={1}, to_apply=%bitcast.214.reduce_sub_computation | reduce | bytes 1966082
  915.3 2.3 reshape.427
  917.6 5.6 all_to_all.51
  923.2 2.9 reshape.428
  926.1 5.1 copy.119
  932.4 2.2 copy.122
  934.7 1.7 copy.147
  (91 shorter events, 17.9 us)
Async XLA Ops:
  7.2 340.4 %copy-start = (bf16[2,192,2560]{2,1,0:T(8,128)(2,1)S(1)}, bf16[2,192,2560]{2,1,0:T(8,128)(2,1)}, u32[]{:S(2)}) copy-start(bf16[2,192,2560]{2,1,0:T(8,128)(2,1)} %param.26) | copy-start | bytes 5898244
  10.4 5.9 copy-start.5
  10.4 35.7 %all-to-all-start = ((f32[8,128,576]{1,2,0:T(8,128)}), f32[8,128,576]{1,2,0:T(8,128)}, u32[]{:S(2)}, u32[]{:S(2)}) async-start(f32[8,128,576]{1,2,0:T(8,128)} %broadcast_in_dim.34), calls=%async_computation | async-start | bytes 4718592 | tf_op jit(solution)/shard_map/all_to_all | solution.py:22
  16.1 32.8 %copy-start.4 = (s32[1,128]{1,0:T(1,128)S(1)}, s32[1,128]{1,0:T(1,128)}, u32[]{:S(2)}) copy-start(s32[1,128]{1,0:T(1,128)} %param.23) | copy-start | bytes 1540
  16.2 97.5 %copy-start.7 = (bf16[1,128,2,576]{1,3,2,0:T(8,128)(2,1)S(1)}, bf16[1,128,2,576]{1,3,2,0:T(8,128)(2,1)}, u32[]{:S(2)}) copy-start(bf16[1,128,2,576]{1,3,2,0:T(8,128)(2,1)} %param.15) | copy-start | bytes 884740
  16.2 97.4 %all-gather.3.cloned.1.call-start = ((), (), s32[]{:S(2)}) async-start(), calls=%async_computation.6 | async-start | bytes 2506752 | tf_op jit(solution)/shard_map/all_gather | solution.py:101
  48.9 160.1 %all-reduce.5.cloned.1.call-start = ((), (), s32[]{:S(2)}) async-start(), calls=%async_computation.7 | async-start | bytes 2621440 | tf_op jit(solution)/shard_map/psum | solution.py:133
  118.3 2.9 copy-start.1
  121.2 1.5 copy-start.2
  121.2 4.3 copy-start.3
  214.7 122.2 %all-to-all-start.1 = ((bf16[32,1,32,2560]{3,2,1,0:T(8,128)(2,1)}), bf16[32,1,32,2560]{3,2,1,0:T(8,128)(2,1)}, u32[]{:S(2)}, u32[]{:S(2)}) async-start(bf16[32,1,32,2560]{3,2,1,0:T(8,128)(2,1)} %bitcast.235), calls=%async_computation.1 | async-start | bytes 10485760 | tf_op jit(solution)/shard_map/all_to_all | solution.py:65
  336.9 4.5 copy-start.6
  341.4 5.4 copy-start.9
  346.8 0.8 copy-start.12
  351.4 12.7 %copy-start.8 = (bf16[2560,32]{0,1:T(8,128)(2,1)S(1)}, bf16[2560,32]{0,1:T(8,128)(2,1)}, u32[]{:S(2)}) copy-start(bf16[2560,32]{0,1:T(8,128)(2,1)} %param.21) | copy-start | bytes 491524
  351.4 125.5 %all-to-all-start.2 = ((bf16[32,1,32,2560]{3,2,1,0:T(8,128)(2,1)}), bf16[32,1,32,2560]{3,2,1,0:T(8,128)(2,1)}, u32[]{:S(2)}, u32[]{:S(2)}) async-start(bf16[32,1,32,2560]{3,2,1,0:T(8,128)(2,1)} %fusion.13), calls=%async_computation.2 | async-start | bytes 10485760 | tf_op jit(solution)/shard_map/all_to_all | solution.py:186
  515.4 309.4 %all-to-all-start.3 = ((bf16[32,1,32,2560]{3,2,1,0:T(8,128)(2,1)}), bf16[32,1,32,2560]{3,2,1,0:T(8,128)(2,1)}, u32[]{:S(2)}, u32[]{:S(2)}) async-start(bf16[32,1,32,2560]{3,2,1,0:T(8,128)(2,1)} %bitcast.236), calls=%async_computation.3 | async-start | bytes 10485760 | tf_op jit(solution)/shard_map/all_to_all | solution.py:65
  525.0 208.5 %all-reduce.9.cloned.1.call-start = ((), (), s32[]{:S(2)}) async-start(), calls=%async_computation.9 | async-start | bytes 655360 | tf_op jit(solution)/shard_map/psum | solution.py:14
  526.4 296.1 %all-reduce.7.cloned.1.call-start = ((), (), s32[]{:S(2)}) async-start(), calls=%async_computation.8 | async-start | bytes 2621440 | tf_op jit(solution)/shard_map/psum | solution.py:192
  530.9 403.8 %all-reduce.11.cloned.1.call-start = ((), (), s32[]{:S(2)}) async-start(), calls=%async_computation.10 | async-start | bytes 655360 | tf_op jit(solution)/shard_map/psum | solution.py:14
  824.8 4.1 copy-start.10
  828.9 3.9 copy-start.11
  881.1 2.5 copy-start.13
Sparse Core Ops, SparseCore 0:
  49.1 64.4 all-gather.2
  122.8 86.1 all-reduce.4
  529.0 204.4 all-reduce.8
  736.0 86.4 all-reduce.6
  824.9 28.3 all-reduce.10
